TPU v7x, 512 devices: a whole 4x4x16 slice. The times are simulated.
512 devices in a mesh: cluster: 16 (over z), vector: 8 (over y, core), replica: 4 (over x).
Axes of the slice: x: 4, y: 4, z: 16, core: 2. Of those that a mesh axis runs over, the one named last changes fastest.
Arguments:
- samples: bfloat16 [128, 524288], P('vector', ('cluster', 'replica')), may hold values from -6 to 6
- leaf_basis_matrix: bfloat16 [32, 64, 8192], P(None, None, ('cluster', 'replica')), may hold values from -0.75 to 0.75
- transfer: bfloat16 [32, 32, 8192], P(None, None, ('cluster', 'replica')), may hold values from -0.75 to 0.75
- leaf_lists: int32 [4, 8192], P(None, ('cluster', 'replica')), may hold values from 0 to 8191, as said below
- leaf_coupling: bfloat16 [32, 32, 4, 8192], P(None, None, None, ('cluster', 'replica')), may hold values from -0.5 to 0.5
- parent_lists: int32 [4, 4096], P(None, ('cluster', 'replica')), may hold values from 0 to 4095, as said below
- parent_coupling: bfloat16 [32, 32, 4, 4096], P(None, None, None, ('cluster', 'replica')), may hold values from -0.5 to 0.5
- test_matrix: bfloat16 [128, 32], P('vector'), may hold values from -0.5 to 0.5
Outputs:
- product: bfloat16 [128, 524288], P('vector', ('cluster', 'replica'))
- new_basis: float32 [64, 32, 8192], P(None, None, ('cluster', 'replica'))
- fresh_transfer_sketch: float32 [32, 32, 8192], P(None, None, ('cluster', 'replica'))
Inputs may be any that keep to these rules, and one draw needn't show every extreme that they name: `leaf_lists`: every source leaf lies within 128 leaves of its target leaf, and some source lies exactly 128 leaves away. `parent_lists`: every source parent lies within half of 128 parents of its target parent, and some source lies exactly that far away.
All inputs are finite; a program needn't handle non-finite values.
Results may differ from a plain program's by a relative error of at most 0.0062.
Values may be sent and summed in bfloat16 or wider, within the bound.
No kernel may reach another device: no remote copies, remote signals or barrier semaphores. Data moves between devices by JAX's collectives and lax.ppermute only.
A program may use at most 64 MiB of HBM per device.

v0:
```python
import jax
import jax.numpy as jnp
from jax import lax
from jax.sharding import PartitionSpec as P


def extended_2(array, sides, width):
    edges = {}
    for axis, dim in sides:
        peers, length = (lax.axis_size(axis), array.shape[dim])
        up = [(i, (i + 1) % peers) for i in range(peers - 1)]
        last = lax.slice_in_dim(array, length - width, length, axis=dim)
        leading = lax.slice_in_dim(array, 0, width, axis=dim)
        edges[dim] = (
            lax.ppermute(last, axis, up),
            lax.ppermute(leading, axis, [(b, a) for a, b in up]),
        )
    done = []
    for _, dim in sides:
        low, high = edges[dim]
        around = [(width, width) if d in done else (0, 0) for d in range(array.ndim)]
        array = jnp.concatenate([jnp.pad(low, around), array, jnp.pad(high, around)], axis=dim)
        done.append(dim)
    return array


def in_order(parts, dim):
    parts = jnp.moveaxis(parts, 0, dim)
    shape = parts.shape
    return parts.reshape(*shape[:dim], shape[dim] * shape[dim + 1], *shape[dim + 2 :])


def sent_to_all(array, axis):
    peers = lax.axis_size(axis)
    return lax.all_to_all(
        jnp.broadcast_to(array[None], (peers, *array.shape)), axis, 0, 0, tiled=True
    )


def gathered_copies(array, axis, dim):
    return in_order(sent_to_all(array, axis), dim)


def in_one_piece(arrays, axis, dim, along):
    both = jnp.concatenate(arrays, axis=along)
    out, at, finished = (gathered_copies(both, axis, dim), 0, [])
    for a in arrays:
        finished.append(lax.slice_in_dim(out, at, at + a.shape[along], axis=along))
        at += a.shape[along]
    return tuple(finished)


def finish_basis(sketch, width):
    scale = lax.rsqrt(jnp.mean(sketch * sketch, axis=0, keepdims=True) + 1e-06)
    new_basis = sketch * scale
    fresh_transfer_sketch = (
        jnp.einsum("pal,pbl->abl", new_basis, sketch, precision=lax.Precision.HIGHEST) / width
    )
    return (new_basis, fresh_transfer_sketch)


def near_take(extended, lists, count):
    first = lax.axis_index(("cluster", "replica")) * count - count
    local_index = lists - first
    return jnp.take(extended, local_index, axis=2)


def shards(
    samples,
    leaf_basis_matrix,
    transfer,
    leaf_lists,
    leaf_coupling,
    parent_lists,
    parent_coupling,
    test_matrix,
):
    rank, width, leaves = leaf_basis_matrix.shape
    vec_local = samples.shape[0]
    each_leaf_amount = samples.reshape(vec_local, leaves, width)
    leaf_coeff = jnp.einsum(
        "rpl,vlp->rvl", leaf_basis_matrix, each_leaf_amount, preferred_element_type=jnp.float32
    ).astype(jnp.bfloat16)
    pairs = transfer.reshape(rank, rank, leaves // 2, 2)
    children = leaf_coeff.reshape(rank, vec_local, leaves // 2, 2)
    parent_coeff = jnp.einsum(
        "abqc,avqc->bvq", pairs, children, preferred_element_type=jnp.float32
    ).astype(jnp.bfloat16)
    leaf_ext = extended_2(leaf_coeff, ((("cluster", "replica"), 2),), leaves)
    leaf_src = near_take(leaf_ext, leaf_lists, leaves)
    parent_ext = extended_2(parent_coeff, ((("cluster", "replica"), 2),), leaves // 2)
    parent_src = near_take(parent_ext, parent_lists, leaves // 2)
    leaf_far = jnp.einsum(
        "rskt,svkt->rvt", leaf_coupling, leaf_src, preferred_element_type=jnp.float32
    )
    parent_far = jnp.einsum(
        "rskq,svkq->rvq", parent_coupling, parent_src, preferred_element_type=jnp.float32
    )
    descend = jnp.einsum(
        "abqc,bvq->avqc", pairs.astype(jnp.float32), parent_far, precision=lax.Precision.HIGHEST
    )
    leaf_count_total = (leaf_far + descend.reshape(rank, vec_local, leaves)).astype(jnp.bfloat16)
    product = jnp.einsum(
        "etw,ebw->bwt", leaf_basis_matrix, leaf_count_total, preferred_element_type=jnp.float32
    ).astype(jnp.bfloat16)
    moved = lax.all_to_all(product, "vector", split_axis=1, concat_axis=0, tiled=True)
    whole_test = gathered_copies(test_matrix, "vector", 0)
    sketch = jnp.einsum("vlp,vr->prl", moved, whole_test, preferred_element_type=jnp.float32)
    shared_basis_rows, shared_transfer_rows = finish_basis(sketch, width)
    new_basis, fresh_transfer_sketch = in_one_piece(
        (shared_basis_rows, shared_transfer_rows), "vector", 2, 0
    )
    return (product.reshape(vec_local, leaves * width), new_basis, fresh_transfer_sketch)


def solution(mesh):
    placed = (
        P("vector", ("cluster", "replica")),
        P(None, None, ("cluster", "replica")),
        P(None, None, ("cluster", "replica")),
        P(None, ("cluster", "replica")),
        P(None, None, None, ("cluster", "replica")),
        P(None, ("cluster", "replica")),
        P(None, None, None, ("cluster", "replica")),
        P("vector", None),
    )
    return jax.shard_map(
        shards,
        mesh=mesh,
        in_specs=placed,
        out_specs=(
            P("vector", ("cluster", "replica")),
            P(None, None, ("cluster", "replica")),
            P(None, None, ("cluster", "replica")),
        ),
        check_vma=False,
    )
```

profile of v0, /device:TPU:256, one launch (start us, length us, event | category | flops | bytes accessed | tf_op | source)
XLA Modules:
  0.0 124.2 jit_solution(8063657740272689346)
XLA Ops:
  0.6 2.5 %copy.69 = bf16[32,64,128]{1,0,2:T(8,128)(2,1)S(1)} copy(bf16[32,64,128]{2,1,0:T(8,128)(2,1)} %param.9) | data formatting | bytes 1048576 | tf_op args[1]
  3.1 1.5 %reshape.45 = bf16[16,128,64]{2,1,0:T(8,128)(2,1)S(1)} reshape(bf16[16,8192]{1,0:T(8,128)(2,1)} %param.8) | data formatting | bytes 524288 | tf_op jit(solution)/shard_map/reshape | solution.py:80
  4.6 1.4 %copy.71 = bf16[32,32,128]{1,0,2:T(8,128)(2,1)S(1)} copy(bf16[32,32,128]{2,1,0:T(8,128)(2,1)S(1)} %copy-done.3) | data formatting | bytes 524288 | tf_op args[2]
  6.1 0.0 copy-start.6
  6.1 0.0 copy-start.5
  6.1 0.0 copy-start.7
  6.1 0.7 convolution_convert_fusion.1
  6.8 0.5 fusion.18
  7.2 0.0 copy-start.2
  7.2 3.4 %collective-permute-start.2 = (bf16[32,16,64]{0,1,2:T(8,128)(2,1)S(1)}, bf16[32,16,64]{0,1,2:T(8,128)(2,1)S(1)}, u32[]{:S(2)}, u32[]{:S(2)}) collective-permute-start(bf16[32,16,64]{0,1,2:T(8,128)(2,1)S(1)} %fusion.18), channel_id=1, source_target_pairs={{0,1},{1,2},{2,3},{3,32},{32,33},{33,34},{34,35},{35,64},{64,65},{... | collective-permute-start | bytes 196616 | tf_op jit(solution)/shard_map/ppermute | solution.py:15
  10.7 5.8 %collective-permute-start.3 = (bf16[32,16,64]{0,1,2:T(8,128)(2,1)S(1)}, bf16[32,16,64]{0,1,2:T(8,128)(2,1)}, u32[]{:S(2)}, u32[]{:S(2)}) collective-permute-start(bf16[32,16,64]{0,1,2:T(8,128)(2,1)S(1)} %fusion.18), channel_id=1, source_target_pairs={{1,0},{2,1},{3,2},{32,3},{33,32},{34,33},{35,34},{64,35},{65,64},{... | collective-permute-start | bytes 196616 | tf_op jit(solution)/shard_map/ppermute | solution.py:16
  16.4 1.9 %collective-permute-start = (bf16[32,16,128]{0,1,2:T(8,128)(2,1)S(1)}, bf16[32,16,128]{0,1,2:T(8,128)(2,1)}, u32[]{:S(2)}, u32[]{:S(2)}) collective-permute-start(bf16[32,16,128]{0,1,2:T(8,128)(2,1)S(1)} %bitcast.94), channel_id=1, source_target_pairs={{0,1},{1,2},{2,3},{3,32},{32,33},{33,34},{34,35},{35,64},{64,65},{... | collective-permute-start | bytes 393224 | tf_op jit(solution)/shard_map/ppermute | solution.py:15
  18.4 7.2 %collective-permute-start.1 = (bf16[32,16,128]{0,1,2:T(8,128)(2,1)S(1)}, bf16[32,16,128]{0,1,2:T(8,128)(2,1)}, u32[]{:S(2)}, u32[]{:S(2)}) collective-permute-start(bf16[32,16,128]{0,1,2:T(8,128)(2,1)S(1)} %bitcast.95), channel_id=1, source_target_pairs={{1,0},{2,1},{3,2},{32,3},{33,32},{34,33},{35,34},{64,35},{65,64},{... | collective-permute-start | bytes 393224 | tf_op jit(solution)/shard_map/ppermute | solution.py:16
  25.6 0.7 reshape.78
  26.3 4.5 %all-to-all-start.1 = ((bf16[8,2,256]{2,1,0:T(2,128)(2,1)}), bf16[8,2,256]{2,1,0:T(2,128)(2,1)S(1)}, u32[]{:S(2)}, u32[]{:S(2)}) async-start(bf16[8,2,256]{2,1,0:T(2,128)(2,1)} %reshape.78), calls=%async_computation.1 | async-start | bytes 16384 | tf_op jit(solution)/shard_map/all_to_all | solution.py:35
  30.9 0.1 reshape.60
  30.9 4.4 %copy.72 = bf16[32,32,4,64]{1,0,3,2:T(8,128)(2,1)} copy(bf16[32,32,4,64]{3,2,1,0:T(4,128)(2,1)} %param.14) | data formatting | bytes 1048576 | tf_op args[6]
  35.4 5.4 %copy.70 = bf16[32,32,4,128]{1,0,3,2:T(8,128)(2,1)} copy(bf16[32,32,4,128]{3,2,1,0:T(4,128)(2,1)} %param.12) | data formatting | bytes 2097152 | tf_op args[4]
  40.8 0.0 copy-start.4
  40.8 0.7 copy-done.4
  41.5 1.3 %pad_maximum_fusion.1 = bf16[32,16,192]{0,1,2:T(8,128)(2,1)S(1)} fusion(bf16[32,16,64]{0,1,2:T(8,128)(2,1)} %collective-permute-done.3, bf16[32,16,64]{0,1,2:T(8,128)(2,1)} %copy-done.2, bf16[32,16,64]{0,1,2:T(8,128)(2,1)} %copy-done.4), kind=kLoop, calls=%fused_computation.24 | loop fusion | flops 196608 | bytes 393216 | tf_op jit(solution)/shard_map/concatenate | solution.py:22
  42.8 1.8 %gather_fusion.1 = bf16[256,32,16]{1,2,0:T(8,128)(2,1)} fusion(bf16[32,16,192]{0,1,2:T(8,128)(2,1)S(1)} %pad_maximum_fusion.1, s32[1024]{0:T(1024)S(1)} %pad_clamp_fusion), kind=kCustom, calls=%fused_computation.1 | custom fusion | bytes 525312 | tf_op jit(solution)/shard_map/jit(_take)/gather | solution.py:65
  44.5 2.6 %convolution_bitcast_fusion = f32[32,16,64,1]{0,1,3,2:T(8,128)S(1)} fusion(bf16[32,32,4,64]{1,0,3,2:T(8,128)(2,1)} %copy.72, bf16[4,64,32,16]{2,3,1,0:T(8,128)(2,1)} %bitcast.99, pred[4,64]{1,0:T(4,128)(4,1)S(1)} %get-tuple-element.15), kind=kOutput, calls=%fused_computation.13 | convolution fusion | flops 8519680 | bytes 917760 | tf_op jit(solution)/shard_map/rskq,svkq->rvq/dot_general | solution.py:96
  47.2 5.2 %fusion.31 = f32[64,16,32,2]{2,1,3,0:T(8,128)} fusion(f32[32,16,64,1]{0,1,3,2:T(8,128)S(1)} %convolution_bitcast_fusion, bf16[32,32,64,2]{1,0,3,2:T(8,128)(2,1)S(1)} %bitcast.89), kind=kOutput, calls=%fused_computation.41 | convolution fusion | flops 25165824 | bytes 655360 | tf_op jit(solution)/shard_map/abqc,bvq->avqc/dot_general | solution.py:99
  52.3 2.7 %pad_maximum_fusion = bf16[32,16,384]{0,1,2:T(8,128)(2,1)} fusion(bf16[32,16,128]{0,1,2:T(8,128)(2,1)} %collective-permute-done.1, bf16[32,16,128]{0,1,2:T(8,128)(2,1)S(1)} %bitcast.96, bf16[32,16,128]{0,1,2:T(8,128)(2,1)} %collective-permute-done), kind=kLoop, calls=%fused_computation.6 | loop fusion | flops 393216 | bytes 786432 | tf_op jit(solution)/shard_map/concatenate | solution.py:22
  55.0 3.8 %gather_fusion = bf16[512,32,16]{1,2,0:T(8,128)(2,1)} fusion(bf16[32,16,384]{0,1,2:T(8,128)(2,1)} %pad_maximum_fusion, s32[1024]{0:T(1024)S(1)} %pad_clamp_fusion.1), kind=kCustom, calls=%fused_computation | custom fusion | bytes 1050624 | tf_op jit(solution)/shard_map/jit(_take)/gather | solution.py:65
  58.8 4.0 %fusion.13 = bf16[16,128,64]{2,0,1:T(8,128)(2,1)S(1)} fusion(bf16[32,64,128]{1,0,2:T(8,128)(2,1)S(1)} %copy.69, f32[32,16,128]{0,1,2:T(8,128)} %bitcast.97, bf16[32,32,4,128]{1,0,3,2:T(8,128)(2,1)} %copy.70, bf16[4,128,32,16]{2,3,1,0:T(8,128)(2,1)} %bitcast.98, pred[4,128]{1,0:T(4,128)(4,1)S(1)} %compare_and_fusion.1), kind=kOutput, calls=%fused_computation.12 | convolution fusion | flops 25690112 | bytes 2621952 | tf_op jit(solution)/shard_map/etw,ebw->bwt/dot_general | solution.py:103
  62.8 0.0 copy-start
  62.8 1.1 reshape.76
  63.9 4.8 %all-to-all-start = ((bf16[8,2,8192]{2,1,0:T(2,128)(2,1)}), bf16[8,2,8192]{2,1,0:T(2,128)(2,1)S(1)}, u32[]{:S(2)}, u32[]{:S(2)}) async-start(bf16[8,2,8192]{2,1,0:T(2,128)(2,1)} %reshape.76), calls=%async_computation | async-start | bytes 524288 | tf_op jit(solution)/shard_map/all_to_all | solution.py:106
  68.7 0.1 reshape.79
  68.8 7.4 %all-to-all-done = bf16[8,2,8192]{2,1,0:T(2,128)(2,1)S(1)} async-done(((bf16[8,2,8192]{2,1,0:T(2,128)(2,1)}), bf16[8,2,8192]{2,1,0:T(2,128)(2,1)S(1)}, u32[]{:S(2)}, u32[]{:S(2)}) %all-to-all-start) | async-done | bytes 262176 | tf_op jit(solution)/shard_map/all_to_all | solution.py:106
  76.2 0.3 reshape.77
  76.6 0.4 multiply_reduce_fusion
  76.9 0.1 broadcast_multiply_fusion
  77.1 0.6 fusion.17
  77.7 0.1 pad_maximum_fusion.2
  77.8 0.2 copy.75
  78.0 1.5 %broadcast_in_dim.44 = f32[8,96,32,16]{1,3,2,0:T(8,128)} broadcast(f32[96,32,16]{0,2,1:T(8,128)S(1)} %copy.75), dimensions={1,2,3} | broadcast | bytes 1769472 | tf_op jit(solution)/shard_map/broadcast_in_dim | solution.py:36
  79.5 3.7 %all-to-all-start.2 = ((f32[8,96,32,16]{1,3,2,0:T(8,128)}), f32[8,96,32,16]{1,3,2,0:T(8,128)S(1)}, u32[]{:S(2)}, u32[]{:S(2)}) async-start(f32[8,96,32,16]{1,3,2,0:T(8,128)} %broadcast_in_dim.44), calls=%async_computation.2 | async-start | bytes 4194304 | tf_op jit(solution)/shard_map/all_to_all | solution.py:35
  83.3 0.1 copy.74
  83.4 1.2 reshape.49
  84.6 25.8 %all-to-all-done.2 = f32[8,96,32,16]{1,3,2,0:T(8,128)S(1)} async-done(((f32[8,96,32,16]{1,3,2,0:T(8,128)}), f32[8,96,32,16]{1,3,2,0:T(8,128)S(1)}, u32[]{:S(2)}, u32[]{:S(2)}) %all-to-all-start.2) | async-done | bytes 1572896 | tf_op jit(solution)/shard_map/all_to_all | solution.py:35
  110.4 2.0 %slice.21 = f32[32,32,8,16]{0,3,1,2:T(8,128)} slice(f32[96,32,8,16]{0,3,1,2:T(8,128)S(1)} %bitcast.86), slice={[64:96], [0:32], [0:8], [0:16]} | slice | bytes 1048576 | tf_op jit(solution)/shard_map/slice | solution.py:48
  112.3 3.9 %copy.77 = f32[32,32,8,16]{1,3,2,0:T(8,128)} copy(f32[32,32,8,16]{0,3,1,2:T(8,128)} %slice.21) | data formatting | bytes 1048576 | tf_op jit(solution)/shard_map/slice | solution.py:48
  116.2 3.0 %copy.79 = f32[32,32,128]{2,1,0:T(8,128)} copy(f32[32,32,128]{1,2,0:T(8,128)} %bitcast.90) | data formatting | bytes 1048576
  119.2 1.6 %copy.76 = f32[64,32,8,16]{0,3,2,1:T(8,128)} copy(f32[64,32,8,16]{0,3,1,2:T(8,128)S(1)} %bitcast.87) | data formatting | bytes 2097152 | tf_op jit(solution)/shard_map/slice | solution.py:48
  120.8 3.4 %copy.78 = f32[64,32,128]{2,1,0:T(8,128)} copy(f32[64,32,128]{0,2,1:T(8,128)} %bitcast.91) | data formatting | bytes 2097152
  (21 shorter events, 0.1 us)
Async XLA Ops:
  0.6 4.0 %copy-start.3 = (bf16[32,32,128]{2,1,0:T(8,128)(2,1)S(1)}, bf16[32,32,128]{2,1,0:T(8,128)(2,1)}, u32[]{:S(2)}) copy-start(bf16[32,32,128]{2,1,0:T(8,128)(2,1)} %param.10) | copy-start | bytes 786436
  6.1 19.5 %copy-start.6 = (bf16[16,32]{1,0:T(8,128)(2,1)S(1)}, bf16[16,32]{1,0:T(8,128)(2,1)}, u32[]{:S(2)}) copy-start(bf16[16,32]{1,0:T(8,128)(2,1)} %param.15) | copy-start | bytes 3076
  6.1 24.7 %copy-start.5 = (s32[4,128]{1,0:T(4,128)S(1)}, s32[4,128]{1,0:T(4,128)}, u32[]{:S(2)}) copy-start(s32[4,128]{1,0:T(4,128)} %param.11) | copy-start | bytes 6148
  6.1 24.7 %copy-start.7 = (s32[4,64]{1,0:T(4,128)S(1)}, s32[4,64]{1,0:T(4,128)}, u32[]{:S(2)}) copy-start(s32[4,64]{1,0:T(4,128)} %param.13) | copy-start | bytes 3076
  7.2 33.5 %copy-start.2 = (bf16[32,16,64]{0,1,2:T(8,128)(2,1)}, bf16[32,16,64]{0,1,2:T(8,128)(2,1)S(1)}, u32[]{:S(2)}) copy-start(bf16[32,16,64]{0,1,2:T(8,128)(2,1)S(1)} %fusion.18) | copy-start | bytes 196612
  7.2 33.5 %collective-permute-start.2 = (bf16[32,16,64]{0,1,2:T(8,128)(2,1)S(1)}, bf16[32,16,64]{0,1,2:T(8,128)(2,1)S(1)}, u32[]{:S(2)}, u32[]{:S(2)}) collective-permute-start(bf16[32,16,64]{0,1,2:T(8,128)(2,1)S(1)} %fusion.18), channel_id=1, source_target_pairs={{0,1},{1,2},{2,3},{3,32},{32,33},{33,34},{34,35},{35,64},{64,65},{... | collective-permute-start | bytes 196616 | tf_op jit(solution)/shard_map/ppermute | solution.py:15
  10.7 30.8 %collective-permute-start.3 = (bf16[32,16,64]{0,1,2:T(8,128)(2,1)S(1)}, bf16[32,16,64]{0,1,2:T(8,128)(2,1)}, u32[]{:S(2)}, u32[]{:S(2)}) collective-permute-start(bf16[32,16,64]{0,1,2:T(8,128)(2,1)S(1)} %fusion.18), channel_id=1, source_target_pairs={{1,0},{2,1},{3,2},{32,3},{33,32},{34,33},{35,34},{64,35},{65,64},{... | collective-permute-start | bytes 196616 | tf_op jit(solution)/shard_map/ppermute | solution.py:16
  16.4 35.9 %collective-permute-start = (bf16[32,16,128]{0,1,2:T(8,128)(2,1)S(1)}, bf16[32,16,128]{0,1,2:T(8,128)(2,1)}, u32[]{:S(2)}, u32[]{:S(2)}) collective-permute-start(bf16[32,16,128]{0,1,2:T(8,128)(2,1)S(1)} %bitcast.94), channel_id=1, source_target_pairs={{0,1},{1,2},{2,3},{3,32},{32,33},{33,34},{34,35},{35,64},{64,65},{... | collective-permute-start | bytes 393224 | tf_op jit(solution)/shard_map/ppermute | solution.py:15
  18.4 34.0 %collective-permute-start.1 = (bf16[32,16,128]{0,1,2:T(8,128)(2,1)S(1)}, bf16[32,16,128]{0,1,2:T(8,128)(2,1)}, u32[]{:S(2)}, u32[]{:S(2)}) collective-permute-start(bf16[32,16,128]{0,1,2:T(8,128)(2,1)S(1)} %bitcast.95), channel_id=1, source_target_pairs={{1,0},{2,1},{3,2},{32,3},{33,32},{34,33},{35,34},{64,35},{65,64},{... | collective-permute-start | bytes 393224 | tf_op jit(solution)/shard_map/ppermute | solution.py:16
  26.3 37.6 %all-to-all-start.1 = ((bf16[8,2,256]{2,1,0:T(2,128)(2,1)}), bf16[8,2,256]{2,1,0:T(2,128)(2,1)S(1)}, u32[]{:S(2)}, u32[]{:S(2)}) async-start(bf16[8,2,256]{2,1,0:T(2,128)(2,1)} %reshape.78), calls=%async_computation.1 | async-start | bytes 16384 | tf_op jit(solution)/shard_map/all_to_all | solution.py:35
  40.8 0.7 copy-start.4
  62.8 14.9 %copy-start = (bf16[16,128,64]{2,0,1:T(8,128)(2,1)}, bf16[16,128,64]{2,0,1:T(8,128)(2,1)S(1)}, u32[]{:S(2)}) copy-start(bf16[16,128,64]{2,0,1:T(8,128)(2,1)S(1)} %fusion.13) | copy-start | bytes 786436
  63.9 12.3 %all-to-all-start = ((bf16[8,2,8192]{2,1,0:T(2,128)(2,1)}), bf16[8,2,8192]{2,1,0:T(2,128)(2,1)S(1)}, u32[]{:S(2)}, u32[]{:S(2)}) async-start(bf16[8,2,8192]{2,1,0:T(2,128)(2,1)} %reshape.76), calls=%async_computation | async-start | bytes 524288 | tf_op jit(solution)/shard_map/all_to_all | solution.py:106
  79.5 3.7 %copy-start.1 = (bf16[16,128,64]{2,0,1:T(8,128)(2,1)S(1)}, bf16[16,128,64]{2,0,1:T(8,128)(2,1)}, u32[]{:S(2)}) copy-start(bf16[16,128,64]{2,0,1:T(8,128)(2,1)} %copy-done) | copy-start | bytes 786436
  79.5 30.8 %all-to-all-start.2 = ((f32[8,96,32,16]{1,3,2,0:T(8,128)}), f32[8,96,32,16]{1,3,2,0:T(8,128)S(1)}, u32[]{:S(2)}, u32[]{:S(2)}) async-start(f32[8,96,32,16]{1,3,2,0:T(8,128)} %broadcast_in_dim.44), calls=%async_computation.2 | async-start | bytes 4194304 | tf_op jit(solution)/shard_map/all_to_all | solution.py:35
where the time goes:
time: 125 us; the launch traced here: 124 us
  local copies, waits for them, and re-layouts  40.6 us (32%)
  waiting for transfers between devices  33.2 us (27%)
  starting transfers between devices  31.3 us (25%)
  matrix products  13.8 us (11%)
  other arithmetic  4.28 us (3%)
    all_to_all x2, waiting for transfers between devices, sent_to_all(): lax.all_to_all(jnp.broadcast_to(array[None], (peers, *array.shape)), axis...  25.8 us
    unnamed x26, local copies, waits for them, and re-layouts  23 us
    ppermute x2, starting transfers between devices, extended_2(): lax.ppermute(leading, axis, [(b, a) for a, b in up])  13 us
    all_to_all x2, starting transfers between devices, sent_to_all(): lax.all_to_all(jnp.broadcast_to(array[None], (peers, *array.shape)), axis...  8.2 us
    slice x3, local copies, waits for them, and re-layouts, in_one_piece(): finished.append(lax.slice_in_dim(out, at, at + a.shape[along], axis=along))  7.48 us
    all_to_all x1, waiting for transfers between devices, shards(): lax.all_to_all(product, 'vector', split_axis=1, concat_axis=0, tiled=True)  7.41 us
    gather x2, local copies, waits for them, and re-layouts, near_take(): return jnp.take(extended, local_index, axis=2)  5.57 us
    ppermute x2, starting transfers between devices, extended_2(): lax.ppermute(last, axis, up)  5.32 us
  transfers between devices with their start and end apart: 7, of which 2 were waited for; matrix products, arithmetic and copies ran while one was open for 28% of the time, Pallas kernels for 0%

commit v1 on v0

--- a/solution.py
+++ b/solution.py
@@ -103,7 +103,12 @@
     product = jnp.einsum(
         "etw,ebw->bwt", leaf_basis_matrix, leaf_count_total, preferred_element_type=jnp.float32
     ).astype(jnp.bfloat16)
-    moved = lax.all_to_all(product, "vector", split_axis=1, concat_axis=0, tiled=True)
+    moved = jnp.concatenate(
+        lax.all_to_all(
+            jnp.stack(jnp.split(product, lax.axis_size("vector"), axis=1)), "vector", 0, 0
+        ),
+        axis=0,
+    )
     whole_test = gathered_copies(test_matrix, "vector", 0)
     sketch = jnp.einsum("vlp,vr->prl", moved, whole_test, preferred_element_type=jnp.float32)
     shared_basis_rows, shared_transfer_rows = finish_basis(sketch, width)

time: 125 us -> 125 us (level)
    unnamed x26 -> x31, local copies, waits for them, and re-layouts: 23 us -> 23.1 us
where the time goes in v1:
time: 125 us; the launch traced here: 124 us
  local copies, waits for them, and re-layouts  40.8 us (33%)
  waiting for transfers between devices  33.2 us (27%)
  starting transfers between devices  31.2 us (25%)
  matrix products  13.6 us (11%)
  other arithmetic  4.37 us (3%)
    all_to_all x2, waiting for transfers between devices, sent_to_all(): lax.all_to_all(jnp.broadcast_to(array[None], (peers, *array.shape)), axis...  25.8 us
    unnamed x31, local copies, waits for them, and re-layouts  23.1 us
    ppermute x2, starting transfers between devices, extended_2(): lax.ppermute(leading, axis, [(b, a) for a, b in up])  13 us
    all_to_all x2, starting transfers between devices, sent_to_all(): lax.all_to_all(jnp.broadcast_to(array[None], (peers, *array.shape)), axis...  8.07 us
    slice x3, local copies, waits for them, and re-layouts, in_one_piece(): finished.append(lax.slice_in_dim(out, at, at + a.shape[along], axis=along))  7.53 us
    all_to_all x1, waiting for transfers between devices, shards(): lax.all_to_all(jnp.stack(jnp.split(product, lax.axis_size('vector'), axis...  7.41 us
    gather x2, local copies, waits for them, and re-layouts, near_take(): return jnp.take(extended, local_index, axis=2)  5.57 us
    ppermute x2, starting transfers between devices, extended_2(): lax.ppermute(last, axis, up)  5.32 us
  transfers between devices with their start and end apart: 7, of which 2 were waited for; matrix products, arithmetic and copies ran while one was open for 28% of the time, Pallas kernels for 0%

profile of v1, /device:TPU:256, one launch (start us, length us, event | category | flops | bytes accessed | tf_op | source)
XLA Modules:
  0.0 124.1 jit_solution(1622782705479816493)
XLA Ops:
  0.6 2.5 %copy.69 = bf16[32,64,128]{1,0,2:T(8,128)(2,1)S(1)} copy(bf16[32,64,128]{2,1,0:T(8,128)(2,1)} %param.9) | data formatting | bytes 1048576 | tf_op args[1]
  3.1 1.5 %reshape.46 = bf16[16,128,64]{2,1,0:T(8,128)(2,1)S(1)} reshape(bf16[16,8192]{1,0:T(8,128)(2,1)} %param.8) | data formatting | bytes 524288 | tf_op jit(solution)/shard_map/reshape | solution.py:80
  4.6 1.4 %copy.71 = bf16[32,32,128]{1,0,2:T(8,128)(2,1)S(1)} copy(bf16[32,32,128]{2,1,0:T(8,128)(2,1)S(1)} %copy-done.2) | data formatting | bytes 524288 | tf_op args[2]
  6.1 0.0 copy-start.5
  6.1 0.0 copy-start.4
  6.1 0.0 copy-start.6
  6.1 0.7 convolution_convert_fusion.1
  6.8 0.5 fusion.18
  7.2 0.0 copy-start.1
  7.2 3.4 %collective-permute-start.2 = (bf16[32,16,64]{0,1,2:T(8,128)(2,1)S(1)}, bf16[32,16,64]{0,1,2:T(8,128)(2,1)S(1)}, u32[]{:S(2)}, u32[]{:S(2)}) collective-permute-start(bf16[32,16,64]{0,1,2:T(8,128)(2,1)S(1)} %fusion.18), channel_id=1, source_target_pairs={{0,1},{1,2},{2,3},{3,32},{32,33},{33,34},{34,35},{35,64},{64,65},{... | collective-permute-start | bytes 196616 | tf_op jit(solution)/shard_map/ppermute | solution.py:15
  10.7 5.8 %collective-permute-start.3 = (bf16[32,16,64]{0,1,2:T(8,128)(2,1)S(1)}, bf16[32,16,64]{0,1,2:T(8,128)(2,1)}, u32[]{:S(2)}, u32[]{:S(2)}) collective-permute-start(bf16[32,16,64]{0,1,2:T(8,128)(2,1)S(1)} %fusion.18), channel_id=1, source_target_pairs={{1,0},{2,1},{3,2},{32,3},{33,32},{34,33},{35,34},{64,35},{65,64},{... | collective-permute-start | bytes 196616 | tf_op jit(solution)/shard_map/ppermute | solution.py:16
  16.4 1.9 %collective-permute-start = (bf16[32,16,128]{0,1,2:T(8,128)(2,1)S(1)}, bf16[32,16,128]{0,1,2:T(8,128)(2,1)}, u32[]{:S(2)}, u32[]{:S(2)}) collective-permute-start(bf16[32,16,128]{0,1,2:T(8,128)(2,1)S(1)} %bitcast.123), channel_id=1, source_target_pairs={{0,1},{1,2},{2,3},{3,32},{32,33},{33,34},{34,35},{35,64},{64,65},{... | collective-permute-start | bytes 393224 | tf_op jit(solution)/shard_map/ppermute | solution.py:15
  18.4 7.2 %collective-permute-start.1 = (bf16[32,16,128]{0,1,2:T(8,128)(2,1)S(1)}, bf16[32,16,128]{0,1,2:T(8,128)(2,1)}, u32[]{:S(2)}, u32[]{:S(2)}) collective-permute-start(bf16[32,16,128]{0,1,2:T(8,128)(2,1)S(1)} %bitcast.124), channel_id=1, source_target_pairs={{1,0},{2,1},{3,2},{32,3},{33,32},{34,33},{35,34},{64,35},{65,64},{... | collective-permute-start | bytes 393224 | tf_op jit(solution)/shard_map/ppermute | solution.py:16
  25.6 0.7 reshape.79
  26.3 4.5 %all-to-all-start.1 = ((bf16[8,2,256]{2,1,0:T(2,128)(2,1)}), bf16[8,2,256]{2,1,0:T(2,128)(2,1)S(1)}, u32[]{:S(2)}, u32[]{:S(2)}) async-start(bf16[8,2,256]{2,1,0:T(2,128)(2,1)} %reshape.79), calls=%async_computation.1 | async-start | bytes 16384 | tf_op jit(solution)/shard_map/all_to_all | solution.py:35
  30.9 0.1 reshape.61
  30.9 4.4 %copy.72 = bf16[32,32,4,64]{1,0,3,2:T(8,128)(2,1)} copy(bf16[32,32,4,64]{3,2,1,0:T(4,128)(2,1)} %param.14) | data formatting | bytes 1048576 | tf_op args[6]
  35.3 5.4 %copy.70 = bf16[32,32,4,128]{1,0,3,2:T(8,128)(2,1)} copy(bf16[32,32,4,128]{3,2,1,0:T(4,128)(2,1)} %param.12) | data formatting | bytes 2097152 | tf_op args[4]
  40.8 0.0 collective-permute-done.2
  40.8 0.0 copy-start.3
  40.8 0.7 copy-done.3
  41.5 1.3 %pad_maximum_fusion.1 = bf16[32,16,192]{0,1,2:T(8,128)(2,1)S(1)} fusion(bf16[32,16,64]{0,1,2:T(8,128)(2,1)} %collective-permute-done.3, bf16[32,16,64]{0,1,2:T(8,128)(2,1)} %copy-done.1, bf16[32,16,64]{0,1,2:T(8,128)(2,1)} %copy-done.3), kind=kLoop, calls=%fused_computation.24 | loop fusion | flops 196608 | bytes 393216 | tf_op jit(solution)/shard_map/concatenate | solution.py:22
  42.8 1.8 %gather_fusion.1 = bf16[256,32,16]{1,2,0:T(8,128)(2,1)} fusion(bf16[32,16,192]{0,1,2:T(8,128)(2,1)S(1)} %pad_maximum_fusion.1, s32[1024]{0:T(1024)S(1)} %pad_clamp_fusion), kind=kCustom, calls=%fused_computation.1 | custom fusion | bytes 525312 | tf_op jit(solution)/shard_map/jit(_take)/gather | solution.py:65
  44.5 2.6 %convolution_bitcast_fusion = f32[32,16,64,1]{0,1,3,2:T(8,128)S(1)} fusion(bf16[32,32,4,64]{1,0,3,2:T(8,128)(2,1)} %copy.72, bf16[4,64,32,16]{2,3,1,0:T(8,128)(2,1)} %bitcast.128, pred[4,64]{1,0:T(4,128)(4,1)S(1)} %get-tuple-element.15), kind=kOutput, calls=%fused_computation.13 | convolution fusion | flops 8519680 | bytes 917760 | tf_op jit(solution)/shard_map/rskq,svkq->rvq/dot_general | solution.py:96
  47.2 5.2 %fusion.40 = f32[64,16,32,2]{2,1,3,0:T(8,128)} fusion(f32[32,16,64,1]{0,1,3,2:T(8,128)S(1)} %convolution_bitcast_fusion, bf16[32,32,64,2]{1,0,3,2:T(8,128)(2,1)S(1)} %bitcast.119), kind=kOutput, calls=%fused_computation.58 | convolution fusion | flops 25165824 | bytes 655360 | tf_op jit(solution)/shard_map/abqc,bvq->avqc/dot_general | solution.py:99
  52.3 2.8 %pad_maximum_fusion = bf16[32,16,384]{0,1,2:T(8,128)(2,1)} fusion(bf16[32,16,128]{0,1,2:T(8,128)(2,1)} %collective-permute-done.1, bf16[32,16,128]{0,1,2:T(8,128)(2,1)S(1)} %bitcast.125, bf16[32,16,128]{0,1,2:T(8,128)(2,1)} %collective-permute-done), kind=kLoop, calls=%fused_computation.6 | loop fusion | flops 393216 | bytes 786432 | tf_op jit(solution)/shard_map/concatenate | solution.py:22
  55.1 3.8 %gather_fusion = bf16[512,32,16]{1,2,0:T(8,128)(2,1)} fusion(bf16[32,16,384]{0,1,2:T(8,128)(2,1)} %pad_maximum_fusion, s32[1024]{0:T(1024)S(1)} %pad_clamp_fusion.1), kind=kCustom, calls=%fused_computation | custom fusion | bytes 1050624 | tf_op jit(solution)/shard_map/jit(_take)/gather | solution.py:65
  58.9 3.8 %fusion.13 = bf16[16,128,64]{2,0,1:T(8,128)(2,1)S(1)} fusion(bf16[32,64,128]{1,0,2:T(8,128)(2,1)S(1)} %copy.69, f32[32,16,128]{0,1,2:T(8,128)S(1)} %bitcast.126, bf16[32,32,4,128]{1,0,3,2:T(8,128)(2,1)} %copy.70, bf16[4,128,32,16]{2,3,1,0:T(8,128)(2,1)} %bitcast.127, pred[4,128]{1,0:T(4,128)(4,1)S(1)} %compare_and_fusion.1), kind=kOutput, calls=%fused_computation.12 | convolution fusion | flops 25690112 | bytes 2621952 | tf_op jit(solution)/shard_map/etw,ebw->bwt/dot_general | solution.py:103
  62.9 1.1 reshape.77
  64.0 4.8 %all-to-all-start = ((bf16[8,2,8192]{2,1,0:T(2,128)(2,1)}), bf16[8,2,8192]{2,1,0:T(2,128)(2,1)S(1)}, u32[]{:S(2)}, u32[]{:S(2)}) async-start(bf16[8,2,8192]{2,1,0:T(2,128)(2,1)} %reshape.77), calls=%async_computation | async-start | bytes 524288 | tf_op jit(solution)/shard_map/all_to_all | solution.py:107
  68.7 0.1 reshape.80
  68.8 7.4 %all-to-all-done = bf16[8,2,8192]{2,1,0:T(2,128)(2,1)S(1)} async-done(((bf16[8,2,8192]{2,1,0:T(2,128)(2,1)}), bf16[8,2,8192]{2,1,0:T(2,128)(2,1)S(1)}, u32[]{:S(2)}, u32[]{:S(2)}) %all-to-all-start) | async-done | bytes 262176 | tf_op jit(solution)/shard_map/all_to_all | solution.py:107
  76.3 0.3 reshape.78
  76.6 0.4 multiply_reduce_fusion
  77.0 0.1 broadcast_multiply_fusion
  77.1 0.6 fusion.17
  77.7 0.1 pad_maximum_fusion.2
  77.9 0.2 copy.75
  78.0 1.5 %broadcast_in_dim.44 = f32[8,96,32,16]{1,3,2,0:T(8,128)} broadcast(f32[96,32,16]{0,2,1:T(8,128)S(1)} %copy.75), dimensions={1,2,3} | broadcast | bytes 1769472 | tf_op jit(solution)/shard_map/broadcast_in_dim | solution.py:36
  79.6 3.6 %all-to-all-start.2 = ((f32[8,96,32,16]{1,3,2,0:T(8,128)}), f32[8,96,32,16]{1,3,2,0:T(8,128)S(1)}, u32[]{:S(2)}, u32[]{:S(2)}) async-start(f32[8,96,32,16]{1,3,2,0:T(8,128)} %broadcast_in_dim.44), calls=%async_computation.2 | async-start | bytes 4194304 | tf_op jit(solution)/shard_map/all_to_all | solution.py:35
  83.2 0.1 copy.74
  83.3 1.2 reshape.50
  84.5 25.8 %all-to-all-done.2 = f32[8,96,32,16]{1,3,2,0:T(8,128)S(1)} async-done(((f32[8,96,32,16]{1,3,2,0:T(8,128)}), f32[8,96,32,16]{1,3,2,0:T(8,128)S(1)}, u32[]{:S(2)}, u32[]{:S(2)}) %all-to-all-start.2) | async-done | bytes 1572896 | tf_op jit(solution)/shard_map/all_to_all | solution.py:35
  110.3 1.9 %slice.21 = f32[32,32,8,16]{0,3,1,2:T(8,128)} slice(f32[96,32,8,16]{0,3,1,2:T(8,128)S(1)} %bitcast.116), slice={[64:96], [0:32], [0:8], [0:16]} | slice | bytes 1048576 | tf_op jit(solution)/shard_map/slice | solution.py:48
  112.2 4.0 %copy.77 = f32[32,32,8,16]{1,3,2,0:T(8,128)} copy(f32[32,32,8,16]{0,3,1,2:T(8,128)} %slice.21) | data formatting | bytes 1048576 | tf_op jit(solution)/shard_map/slice | solution.py:48
  116.2 3.0 %copy.79 = f32[32,32,128]{2,1,0:T(8,128)} copy(f32[32,32,128]{1,2,0:T(8,128)} %bitcast.120) | data formatting | bytes 1048576
  119.1 1.6 %copy.76 = f32[64,32,8,16]{0,3,2,1:T(8,128)} copy(f32[64,32,8,16]{0,3,1,2:T(8,128)S(1)} %bitcast.117) | data formatting | bytes 2097152 | tf_op jit(solution)/shard_map/slice | solution.py:48
  120.7 3.4 %copy.78 = f32[64,32,128]{2,1,0:T(8,128)} copy(f32[64,32,128]{0,2,1:T(8,128)} %bitcast.121) | data formatting | bytes 2097152
  (27 shorter events, 0.2 us)
Async XLA Ops:
  0.6 4.0 %copy-start.2 = (bf16[32,32,128]{2,1,0:T(8,128)(2,1)S(1)}, bf16[32,32,128]{2,1,0:T(8,128)(2,1)}, u32[]{:S(2)}) copy-start(bf16[32,32,128]{2,1,0:T(8,128)(2,1)} %param.10) | copy-start | bytes 786436
  6.1 19.5 %copy-start.5 = (bf16[16,32]{1,0:T(8,128)(2,1)S(1)}, bf16[16,32]{1,0:T(8,128)(2,1)}, u32[]{:S(2)}) copy-start(bf16[16,32]{1,0:T(8,128)(2,1)} %param.15) | copy-start | bytes 3076
  6.1 24.7 %copy-start.4 = (s32[4,128]{1,0:T(4,128)S(1)}, s32[4,128]{1,0:T(4,128)}, u32[]{:S(2)}) copy-start(s32[4,128]{1,0:T(4,128)} %param.11) | copy-start | bytes 6148
  6.1 24.7 %copy-start.6 = (s32[4,64]{1,0:T(4,128)S(1)}, s32[4,64]{1,0:T(4,128)}, u32[]{:S(2)}) copy-start(s32[4,64]{1,0:T(4,128)} %param.13) | copy-start | bytes 3076
  7.2 33.5 %copy-start.1 = (bf16[32,16,64]{0,1,2:T(8,128)(2,1)}, bf16[32,16,64]{0,1,2:T(8,128)(2,1)S(1)}, u32[]{:S(2)}) copy-start(bf16[32,16,64]{0,1,2:T(8,128)(2,1)S(1)} %fusion.18) | copy-start | bytes 196612
  7.2 33.5 %collective-permute-start.2 = (bf16[32,16,64]{0,1,2:T(8,128)(2,1)S(1)}, bf16[32,16,64]{0,1,2:T(8,128)(2,1)S(1)}, u32[]{:S(2)}, u32[]{:S(2)}) collective-permute-start(bf16[32,16,64]{0,1,2:T(8,128)(2,1)S(1)} %fusion.18), channel_id=1, source_target_pairs={{0,1},{1,2},{2,3},{3,32},{32,33},{33,34},{34,35},{35,64},{64,65},{... | collective-permute-start | bytes 196616 | tf_op jit(solution)/shard_map/ppermute | solution.py:15
  10.7 30.8 %collective-permute-start.3 = (bf16[32,16,64]{0,1,2:T(8,128)(2,1)S(1)}, bf16[32,16,64]{0,1,2:T(8,128)(2,1)}, u32[]{:S(2)}, u32[]{:S(2)}) collective-permute-start(bf16[32,16,64]{0,1,2:T(8,128)(2,1)S(1)} %fusion.18), channel_id=1, source_target_pairs={{1,0},{2,1},{3,2},{32,3},{33,32},{34,33},{35,34},{64,35},{65,64},{... | collective-permute-start | bytes 196616 | tf_op jit(solution)/shard_map/ppermute | solution.py:16
  16.4 35.9 %collective-permute-start = (bf16[32,16,128]{0,1,2:T(8,128)(2,1)S(1)}, bf16[32,16,128]{0,1,2:T(8,128)(2,1)}, u32[]{:S(2)}, u32[]{:S(2)}) collective-permute-start(bf16[32,16,128]{0,1,2:T(8,128)(2,1)S(1)} %bitcast.123), channel_id=1, source_target_pairs={{0,1},{1,2},{2,3},{3,32},{32,33},{33,34},{34,35},{35,64},{64,65},{... | collective-permute-start | bytes 393224 | tf_op jit(solution)/shard_map/ppermute | solution.py:15
  18.4 34.0 %collective-permute-start.1 = (bf16[32,16,128]{0,1,2:T(8,128)(2,1)S(1)}, bf16[32,16,128]{0,1,2:T(8,128)(2,1)}, u32[]{:S(2)}, u32[]{:S(2)}) collective-permute-start(bf16[32,16,128]{0,1,2:T(8,128)(2,1)S(1)} %bitcast.124), channel_id=1, source_target_pairs={{1,0},{2,1},{3,2},{32,3},{33,32},{34,33},{35,34},{64,35},{65,64},{... | collective-permute-start | bytes 393224 | tf_op jit(solution)/shard_map/ppermute | solution.py:16
  26.3 37.6 %all-to-all-start.1 = ((bf16[8,2,256]{2,1,0:T(2,128)(2,1)}), bf16[8,2,256]{2,1,0:T(2,128)(2,1)S(1)}, u32[]{:S(2)}, u32[]{:S(2)}) async-start(bf16[8,2,256]{2,1,0:T(2,128)(2,1)} %reshape.79), calls=%async_computation.1 | async-start | bytes 16384 | tf_op jit(solution)/shard_map/all_to_all | solution.py:35
  40.8 0.7 copy-start.3
  52.3 6.6 %copy-start = (f32[64,16,32,2]{2,1,3,0:T(8,128)S(1)}, f32[64,16,32,2]{2,1,3,0:T(8,128)}, u32[]{:S(2)}) copy-start(f32[64,16,32,2]{2,1,3,0:T(8,128)} %fusion.40) | copy-start | bytes 786436
  64.0 12.3 %all-to-all-start = ((bf16[8,2,8192]{2,1,0:T(2,128)(2,1)}), bf16[8,2,8192]{2,1,0:T(2,128)(2,1)S(1)}, u32[]{:S(2)}, u32[]{:S(2)}) async-start(bf16[8,2,8192]{2,1,0:T(2,128)(2,1)} %reshape.77), calls=%async_computation | async-start | bytes 524288 | tf_op jit(solution)/shard_map/all_to_all | solution.py:107
  79.6 30.7 %all-to-all-start.2 = ((f32[8,96,32,16]{1,3,2,0:T(8,128)}), f32[8,96,32,16]{1,3,2,0:T(8,128)S(1)}, u32[]{:S(2)}, u32[]{:S(2)}) async-start(f32[8,96,32,16]{1,3,2,0:T(8,128)} %broadcast_in_dim.44), calls=%async_computation.2 | async-start | bytes 4194304 | tf_op jit(solution)/shard_map/all_to_all | solution.py:35
